TPU v7x, 32 devices: a whole 2x2x4 slice. The times are simulated.
32 devices in a mesh: rep: 4 (over y, x), shard: 8 (over z, core).
Axes of the slice: x: 2, y: 2, z: 4, core: 2. Of those that a mesh axis runs over, the one named last changes fastest.
Arguments:
- hidden_in: float32 [4096, 768], P(('rep', 'shard')), may hold values from -6 to 6
- doc_ids: int32 [32, 128], P(('rep', 'shard')), may hold values from 0 to 3, never falling along the last dimension, each value on 1 to 64 neighbouring positions
- cotangent: float32 [4096, 768], P(('rep', 'shard')), may hold values from -6 to 6
- pre_gain: float32 [1, 768], P(None, 'shard'), may hold values from 0.25 to 1.75
- pre_shift: float32 [1, 768], P(None, 'shard'), may hold values from -3 to 3
- qkv_weight: float32 [1, 768, 2304], P(None, 'shard'), may hold values from -0.21875 to 0.21875
- query_bias: float32 [1, 768], P(None, 'shard'), may hold values from -3 to 3
- value_bias: float32 [1, 768], P(None, 'shard'), may hold values from -3 to 3
- out_weight: float32 [1, 768, 768], P(None, 'shard'), may hold values from -0.875 to 0.875
- out_bias: float32 [1, 768], P(None, 'shard'), may hold values from -3 to 3
- post_gain: float32 [1, 768], P(None, 'shard'), may hold values from 0.25 to 1.75
- post_shift: float32 [1, 768], P(None, 'shard'), may hold values from -3 to 3
- up_weight: float32 [1, 768, 3072], P(None, 'shard'), may hold values from -0.21875 to 0.21875
- up_bias: float32 [1, 3072], P(None, 'shard'), may hold values from -3 to 3
- down_weight: float32 [1, 3072, 768], P(None, 'shard'), may hold values from -0.109375 to 0.109375
- down_bias: float32 [1, 768], P(None, 'shard'), may hold values from -3 to 3
Outputs:
- hidden_out: float32 [4096, 768], P(('rep', 'shard'))
- input_grad: float32 [4096, 768], P(('rep', 'shard'))
- grad_pre_gain: float32 [1, 768], P(None, 'shard')
- grad_pre_shift: float32 [1, 768], P(None, 'shard')
- grad_qkv_weight: float32 [1, 768, 2304], P(None, 'shard')
- grad_query_bias: float32 [1, 768], P(None, 'shard')
- grad_value_bias: float32 [1, 768], P(None, 'shard')
- grad_out_weight: float32 [1, 768, 768], P(None, 'shard')
- grad_out_bias: float32 [1, 768], P(None, 'shard')
- grad_post_gain: float32 [1, 768], P(None, 'shard')
- grad_post_shift: float32 [1, 768], P(None, 'shard')
- grad_up_weight: float32 [1, 768, 3072], P(None, 'shard')
- grad_up_bias: float32 [1, 3072], P(None, 'shard')
- grad_down_weight: float32 [1, 3072, 768], P(None, 'shard')
- grad_down_bias: float32 [1, 768], P(None, 'shard')
Inputs may be any that keep to these rules, and one draw needn't show every extreme that they name: `doc_ids`: along each row the document number never falls; all 4 documents appear in every row, each of 1 to 64 tokens, one of exactly 64.
All inputs are finite; a program needn't handle non-finite values.
Results may differ from a plain program's by a relative error of at most 0.018.
Values may be sent and summed in bfloat16 or wider, within the bound.
No kernel may reach another device: no remote copies, remote signals or barrier semaphores. Data moves between devices by JAX's collectives and lax.ppermute only.
A program may use at most 128 MiB of HBM per device.

v0:
```python
import jax
import jax.numpy as jnp
from jax import lax
from jax.sharding import PartitionSpec as P

HEADS = 12
HEAD = 64
LAYERS = 1
EPS = 1e-05
GELU_C = 0.7978845608028654
NEG_FILL = -1e30


def norm(values_in, gains, shifts):
    average = jnp.mean(values_in, axis=-1, keepdims=True)
    centred = values_in - average
    spread = jnp.mean(centred * centred, axis=-1, keepdims=True)
    return centred * lax.rsqrt(spread + EPS) * gains + shifts


def gelu_tanh(values_in):
    return (
        0.5
        * values_in
        * (1.0 + jnp.tanh(GELU_C * (values_in + 0.044715 * values_in * values_in * values_in)))
    )


def project(left, right):
    return jnp.dot(left, right, preferred_element_type=jnp.float32)


def project_back(left, right):
    return lax.dot_general(
        left, right, (((0,), (0,)), ((), ())), preferred_element_type=jnp.float32
    )


def project_trans(left, right):
    return lax.dot_general(
        left, right, (((1,), (1,)), ((), ())), preferred_element_type=jnp.float32
    )


def layer_slices(shards, layer_index):
    return tuple((stacked[layer_index].astype(jnp.bfloat16) for stacked in shards))


def fetch_forward(shards, layer_index):
    parts = layer_slices(shards, layer_index)
    return (
        lax.all_gather(parts[0], "shard", axis=0, tiled=True),
        lax.all_gather(parts[1], "shard", axis=0, tiled=True),
        lax.all_gather(parts[2], "shard", axis=0, tiled=True),
        lax.all_gather(parts[3], "shard", axis=0, tiled=True),
        lax.all_gather(parts[4], "shard", axis=0, tiled=True),
        lax.all_gather(parts[5], "shard", axis=0, tiled=True),
        lax.all_gather(parts[6], "shard", axis=0, tiled=True),
        lax.all_gather(parts[7], "shard", axis=0, tiled=True),
        lax.all_gather(parts[8], "shard", axis=0, tiled=True),
        lax.all_gather(parts[9], "shard", axis=0, tiled=True),
        lax.all_gather(parts[10], "shard", axis=0, tiled=True),
        lax.all_gather(parts[11], "shard", axis=0, tiled=True),
        lax.all_gather(parts[12], "shard", axis=0, tiled=True),
    )


def reduce_nested_rest(grads):
    owned = (
        lax.psum_scatter(
            grads[0].astype(jnp.bfloat16), "shard", scatter_dimension=0, tiled=True
        ).astype(jnp.float32),
        lax.psum_scatter(
            grads[1].astype(jnp.bfloat16), "shard", scatter_dimension=0, tiled=True
        ).astype(jnp.float32),
        lax.psum_scatter(
            grads[2].astype(jnp.bfloat16), "shard", scatter_dimension=0, tiled=True
        ).astype(jnp.float32),
        lax.psum_scatter(
            grads[3].astype(jnp.bfloat16), "shard", scatter_dimension=0, tiled=True
        ).astype(jnp.float32),
        lax.psum_scatter(
            grads[4].astype(jnp.bfloat16), "shard", scatter_dimension=0, tiled=True
        ).astype(jnp.float32),
        lax.psum_scatter(
            grads[5].astype(jnp.bfloat16), "shard", scatter_dimension=0, tiled=True
        ).astype(jnp.float32),
        lax.psum_scatter(
            grads[6].astype(jnp.bfloat16), "shard", scatter_dimension=0, tiled=True
        ).astype(jnp.float32),
        lax.psum_scatter(
            grads[7].astype(jnp.bfloat16), "shard", scatter_dimension=0, tiled=True
        ).astype(jnp.float32),
        lax.psum_scatter(
            grads[8].astype(jnp.bfloat16), "shard", scatter_dimension=0, tiled=True
        ).astype(jnp.float32),
        lax.psum_scatter(
            grads[9].astype(jnp.bfloat16), "shard", scatter_dimension=0, tiled=True
        ).astype(jnp.float32),
        lax.psum_scatter(
            grads[10].astype(jnp.bfloat16), "shard", scatter_dimension=0, tiled=True
        ).astype(jnp.float32),
    )
    return (
        lax.psum(owned[0].astype(jnp.bfloat16), "rep").astype(jnp.float32),
        lax.psum(owned[1].astype(jnp.bfloat16), "rep").astype(jnp.float32),
        lax.psum(owned[2].astype(jnp.bfloat16), "rep").astype(jnp.float32),
        lax.psum(owned[3].astype(jnp.bfloat16), "rep").astype(jnp.float32),
        lax.psum(owned[4].astype(jnp.bfloat16), "rep").astype(jnp.float32),
        lax.psum(owned[5].astype(jnp.bfloat16), "rep").astype(jnp.float32),
        lax.psum(owned[6].astype(jnp.bfloat16), "rep").astype(jnp.float32),
        lax.psum(owned[7].astype(jnp.bfloat16), "rep").astype(jnp.float32),
        lax.psum(owned[8].astype(jnp.bfloat16), "rep").astype(jnp.float32),
        lax.psum(owned[9].astype(jnp.bfloat16), "rep").astype(jnp.float32),
        lax.psum(owned[10].astype(jnp.bfloat16), "rep").astype(jnp.float32),
    )


def block_scores(query_block, key_rows, doc_block, doc_row, offset):
    query_places = offset + lax.iota(jnp.int32, query_block.shape[0])
    key_places = lax.iota(jnp.int32, key_rows.shape[0])
    allowed = (query_places[:, None] >= key_places[None, :]) & (
        doc_block[:, None] == doc_row[None, :]
    )
    scores = (
        jnp.einsum("qhe,khe->hqk", query_block, key_rows, preferred_element_type=jnp.float32)
        * 0.125
    )
    return jnp.where(allowed[None], scores, NEG_FILL)


def attention_forward(queries, key_rows, value_rows, doc_row):
    length = queries.shape[0]
    rows_block = min(length, 512)
    blocks = length // rows_block

    def one_block(block_index):
        offset = block_index * rows_block
        scores = block_scores(queries, key_rows, doc_row, doc_row, offset)
        highest = jnp.max(scores, axis=-1, keepdims=True)
        log_total = highest + jnp.log(jnp.sum(jnp.exp(scores - highest), axis=-1, keepdims=True))
        weights = jnp.exp(scores - log_total).astype(jnp.bfloat16)
        mixed = jnp.einsum("hqk,khe->qhe", weights, value_rows, preferred_element_type=jnp.float32)
        return (mixed.astype(jnp.bfloat16), log_total)

    mixed, log_totals = lax.map(one_block, jnp.arange(blocks, dtype=jnp.int32))
    return (mixed.reshape(length, -1), log_totals)


def attention_backward(queries, key_rows, value_rows, doc_row, log_totals, grad_mixed):
    length = queries.shape[0]
    rows_block = min(length, 512)
    blocks = length // rows_block

    def one_block(carry, block_index):
        grad_keys, grad_values = carry
        offset = block_index * rows_block
        scores = block_scores(queries, key_rows, doc_row, doc_row, offset)
        weights = jnp.exp(scores - log_totals[block_index])
        grad_values = grad_values + jnp.einsum(
            "hqk,qhe->khe",
            weights.astype(jnp.bfloat16),
            grad_mixed,
            preferred_element_type=jnp.float32,
        )
        grad_weights = jnp.einsum(
            "qhe,khe->hqk", grad_mixed, value_rows, preferred_element_type=jnp.float32
        )
        grad_scores = weights * (
            grad_weights - jnp.sum(grad_weights * weights, axis=-1, keepdims=True)
        )
        grad_scores = grad_scores.astype(jnp.bfloat16)
        grad_query = (
            jnp.einsum("hqk,khe->qhe", grad_scores, key_rows, preferred_element_type=jnp.float32)
            * 0.125
        )
        grad_keys = (
            grad_keys
            + jnp.einsum("hqk,qhe->khe", grad_scores, queries, preferred_element_type=jnp.float32)
            * 0.125
        )
        return ((grad_keys, grad_values), grad_query)

    zeros_kv = jnp.zeros(key_rows.shape, jnp.float32)
    (grad_keys, grad_values), grad_queries = lax.scan(
        one_block, (zeros_kv, zeros_kv), jnp.arange(blocks, dtype=jnp.int32)
    )
    return (
        grad_queries.reshape(length, -1),
        grad_keys.reshape(length, -1),
        grad_values.reshape(length, -1),
    )


def layer_forward(hidden, weights, doc_row):
    (
        pre_gain,
        pre_shift,
        qkv_weight,
        query_bias,
        value_bias,
        out_weight,
        out_bias,
        post_gain,
        post_shift,
        up_weight,
        up_bias,
        down_weight,
        down_bias,
    ) = weights
    rows_here = hidden.shape[0]
    normed = norm(hidden, pre_gain.astype(jnp.float32), pre_shift.astype(jnp.float32)).astype(
        jnp.bfloat16
    )
    bias_row = jnp.concatenate([query_bias, jnp.zeros_like(query_bias), value_bias]).astype(
        jnp.float32
    )
    packed = (project(normed, qkv_weight) + bias_row).astype(jnp.bfloat16)
    shaped = packed.reshape(rows_here, 3, HEADS, HEAD)
    mixed, log_totals = attention_forward(shaped[:, 0], shaped[:, 1], shaped[:, 2], doc_row)
    middle = hidden + project(mixed, out_weight) + out_bias.astype(jnp.float32)
    normed_two = norm(middle, post_gain.astype(jnp.float32), post_shift.astype(jnp.float32)).astype(
        jnp.bfloat16
    )
    pre_act = project(normed_two, up_weight) + up_bias.astype(jnp.float32)
    activ = gelu_tanh(pre_act).astype(jnp.bfloat16)
    output = middle + project(activ, down_weight) + down_bias.astype(jnp.float32)
    stored = (hidden, normed, packed, mixed, log_totals, middle, normed_two, pre_act, activ)
    return (output, stored)


def layer_backward(grad_out, weights, stored, doc_row):
    (
        pre_gain,
        pre_shift,
        qkv_weight,
        query_bias,
        value_bias,
        out_weight,
        out_bias,
        post_gain,
        post_shift,
        up_weight,
        up_bias,
        down_weight,
        down_bias,
    ) = weights
    hidden, normed, packed, mixed, log_totals, middle, normed_two, pre_act, activ = stored
    rows_here, width = hidden.shape
    grad_down = grad_out.astype(jnp.bfloat16)
    activ_columns = lax.all_to_all(activ, "shard", split_axis=1, concat_axis=0, tiled=True)
    group_grads = lax.all_gather(grad_down, "shard", axis=0, tiled=True)
    grad_down_weight = project_back(activ_columns, group_grads)
    width_part = width // lax.axis_size("shard")
    column_total = jnp.sum(group_grads.astype(jnp.float32), axis=0)
    grad_down_bias = lax.dynamic_slice_in_dim(
        column_total, lax.axis_index("shard") * width_part, width_part, 0
    )
    grad_activ = project_trans(grad_down, down_weight)
    unused_gelu, gelu_pull = jax.vjp(gelu_tanh, pre_act)
    grad_pre = gelu_pull(grad_activ)[0].astype(jnp.bfloat16)
    grad_up_weight = project_back(normed_two, grad_pre)
    grad_up_bias = jnp.sum(grad_pre.astype(jnp.float32), axis=0)
    grad_normed_two = project_trans(grad_pre, up_weight)
    unused_post, post_pull = jax.vjp(
        norm, middle, post_gain.astype(jnp.float32), post_shift.astype(jnp.float32)
    )
    grad_middle, grad_post_gain, grad_post_shift = post_pull(grad_normed_two)
    grad_middle = grad_middle + grad_out
    grad_attn = grad_middle.astype(jnp.bfloat16)
    grad_out_weight = project_back(mixed, grad_attn)
    grad_out_bias = jnp.sum(grad_attn.astype(jnp.float32), axis=0)
    grad_mixed = (
        project_trans(grad_attn, out_weight).astype(jnp.bfloat16).reshape(rows_here, HEADS, HEAD)
    )
    shaped = packed.reshape(rows_here, 3, HEADS, HEAD)
    grad_queries, grad_keys, grad_values = attention_backward(
        shaped[:, 0], shaped[:, 1], shaped[:, 2], doc_row, log_totals, grad_mixed
    )
    grad_packed = jnp.concatenate([grad_queries, grad_keys, grad_values], axis=1).astype(
        jnp.bfloat16
    )
    grad_qkv_weight = project_back(normed, grad_packed)
    column_sums = jnp.sum(grad_packed.astype(jnp.float32), axis=0)
    grad_query_bias = column_sums[:width]
    grad_value_bias = column_sums[2 * width :]
    grad_normed = project_trans(grad_packed, qkv_weight)
    unused_pre, pre_pull = jax.vjp(
        norm, hidden, pre_gain.astype(jnp.float32), pre_shift.astype(jnp.float32)
    )
    grad_hidden, grad_pre_gain, grad_pre_shift = pre_pull(grad_normed)
    grads = (
        grad_pre_gain,
        grad_pre_shift,
        grad_qkv_weight,
        grad_query_bias,
        grad_value_bias,
        grad_out_weight,
        grad_out_bias,
        grad_post_gain,
        grad_post_shift,
        grad_up_weight,
        grad_up_bias,
        grad_down_weight,
        grad_down_bias,
    )
    return (grad_hidden + grad_middle, grads)


def on_device(
    hidden_in,
    doc_ids,
    cotangent,
    pre_gain,
    pre_shift,
    qkv_weight,
    query_bias,
    value_bias,
    out_weight,
    out_bias,
    post_gain,
    post_shift,
    up_weight,
    up_bias,
    down_weight,
    down_bias,
):
    shards = (
        pre_gain,
        pre_shift,
        qkv_weight,
        query_bias,
        value_bias,
        out_weight,
        out_bias,
        post_gain,
        post_shift,
        up_weight,
        up_bias,
        down_weight,
        down_bias,
    )
    doc_row = doc_ids[0]
    hidden = hidden_in
    layer_index = 0
    weights = fetch_forward(shards, layer_index)
    hidden, stored = layer_forward(hidden, weights, doc_row)
    gathered_all = [weights]
    stored_all = [stored]
    grad_flow = cotangent
    reduced_all = [None] * LAYERS
    for layer_index in reversed(range(LAYERS)):
        weights = gathered_all[layer_index]
        grad_flow, layer_grads = layer_backward(
            grad_flow, weights, stored_all[layer_index], doc_row
        )
        rest_grads = tuple((layer_grads[member] for member in range(11)))
        rest_sums = reduce_nested_rest(rest_grads)
        down_pair = (layer_grads[11], layer_grads[12])
        down_sums = (
            lax.psum(down_pair[0].astype(jnp.bfloat16), "rep").astype(jnp.float32),
            lax.psum(down_pair[1].astype(jnp.bfloat16), "rep").astype(jnp.float32),
        )
        reduced_all[layer_index] = tuple(rest_sums) + tuple(down_sums)
    stacked = tuple((jnp.stack([reduced_all[0][member]]) for member in range(13)))
    return (
        hidden,
        grad_flow,
        stacked[0],
        stacked[1],
        stacked[2],
        stacked[3],
        stacked[4],
        stacked[5],
        stacked[6],
        stacked[7],
        stacked[8],
        stacked[9],
        stacked[10],
        stacked[11],
        stacked[12],
    )


def solution(mesh):
    in_specs = (
        P(("rep", "shard"), None),
        P(("rep", "shard"), None),
        P(("rep", "shard"), None),
        P(None, "shard"),
        P(None, "shard"),
        P(None, "shard", None),
        P(None, "shard"),
        P(None, "shard"),
        P(None, "shard", None),
        P(None, "shard"),
        P(None, "shard"),
        P(None, "shard"),
        P(None, "shard", None),
        P(None, "shard"),
        P(None, "shard", None),
        P(None, "shard"),
    )
    out_specs = (
        P(("rep", "shard"), None),
        P(("rep", "shard"), None),
        P(None, "shard"),
        P(None, "shard"),
        P(None, "shard", None),
        P(None, "shard"),
        P(None, "shard"),
        P(None, "shard", None),
        P(None, "shard"),
        P(None, "shard"),
        P(None, "shard"),
        P(None, "shard", None),
        P(None, "shard"),
        P(None, "shard", None),
        P(None, "shard"),
    )
    return jax.shard_map(
        on_device, mesh=mesh, in_specs=in_specs, out_specs=out_specs, check_vma=False
    )
```

profile of v0, /device:TPU:0, one launch (start us, length us, event | category | flops | bytes accessed | tf_op | source)
XLA Modules:
  0.0 431.4 jit_solution(6924387649990992)
XLA Ops:
  7.2 2.1 convert_element_type.231
  9.4 0.7 convert_element_type.242
  10.2 0.9 convert_element_type.254
  11.3 0.9 convert_element_type.260
  12.2 0.7 convert_element_type.265
  13.2 0.6 fusion.54
  15.9 32.5 %all-reduce.17 = (bf16[768]{0:T(1024)(128)(2,1)S(1)}, bf16[768]{0:T(1024)(128)(2,1)S(1)}, bf16[768]{0:T(1024)(128)(2,1)S(1)}, bf16[768]{0:T(1024)(128)(2,1)S(1)}...) all-reduce(bf16[768]{0:T(1024)(128)(2,1)S(1)} %dynamic-update-slice, ...), channel_id=6, replica_groups=mesh['rep'=4,'shard'=8] {'shard'}, use_global_device_ids=true, to_apply=%add.3 | all-reduce | flops 5376 | bytes 21504 | tf_op jit(solution)/shard_map/all_gather | solution.py:56
  48.9 12.8 %all-gather.10 = bf16[1,3072]{1,0:T(2,128)(2,1)S(1)} all-gather(bf16[1,384]{1,0:T(2,128)(2,1)S(1)} %convert_element_type.256), channel_id=12, replica_groups=mesh['rep'=4,'shard'=8] {'shard'}, dimensions={1}, use_global_device_ids=true | all-gather | bytes 6912 | tf_op jit(solution)/shard_map/all_gather | solution.py:62
  61.8 2.8 fusion.11
  65.7 13.2 %all-gather.23.cloned.1.call-done = bf16[1,768,768]{2,1,0:T(8,128)(2,1)} async-done(((bf16[1,96,768]{2,1,0:T(8,128)(2,1)}), bf16[1,768,768]{2,1,0:T(8,128)(2,1)}) %all-gather.23.cloned.1.call-update) | async-done | bytes 1179664 | tf_op jit(solution)/shard_map/all_gather | solution.py:57
  78.9 1.7 fusion.56
  80.8 51.2 %all-gather.25.cloned.1.call-done = bf16[1,768,3072]{2,1,0:T(8,128)(2,1)} async-done(((bf16[1,96,3072]{2,1,0:T(8,128)(2,1)}), bf16[1,768,3072]{2,1,0:T(8,128)(2,1)}) %all-gather.25.cloned.1.call-update) | async-done | bytes 4718608 | tf_op jit(solution)/shard_map/all_gather | solution.py:61
  132.0 5.1 %multiply_convert_fusion = (bf16[128,3072]{1,0:T(8,128)(2,1)}, f32[128,3072]{1,0:T(8,128)}) fusion(f32[3072]{0:T(1024)S(1)} %bitcast.156, bf16[1,768,3072]{2,1,0:T(8,128)(2,1)} %all-gather.25.cloned.1.call-done, f32[128,768]{1,0:T(8,128)S(1)} %get-tuple-element.114, f32[768]{0:T(1024)S(1)} %convert_element_type.292, f32[768]{0:T(1024)S(1)} %convert_element_type.291, ...), kind=kOutput, calls=%fused_computation.27 | convolution fusion | flops 608403456 | bytes 7490560 | tf_op jit(solution)/shard_map/dot_general | solution.py:30
  137.1 47.0 %all-gather.27.cloned.1.call-done = bf16[1,3072,768]{2,1,0:T(8,128)(2,1)} async-done(((bf16[1,384,768]{2,1,0:T(8,128)(2,1)}), bf16[1,3072,768]{2,1,0:T(8,128)(2,1)}) %all-gather.27.cloned.1.call-update) | async-done | bytes 4718608 | tf_op jit(solution)/shard_map/all_gather | solution.py:63
  184.1 5.9 %fusion.57 = (bf16[3072]{0:T(1024)(128)(2,1)}, bf16[128,3072]{1,0:T(8,128)(2,1)S(1)}) fusion(f32[128,3072]{1,0:T(8,128)} %get-tuple-element.116, bf16[128,768]{1,0:T(8,128)(2,1)S(1)} %copy-done.17, bf16[1,3072,768]{2,1,0:T(8,128)(2,1)} %all-gather.27.cloned.1.call-done), kind=kOutput, calls=%fused_computation.109 | convolution fusion | flops 613807104 | bytes 7280640 | tf_op jit(solution)/shard_map/dot_general | solution.py:40
  190.0 2.3 multiply_reduce_fusion.1
  193.1 0.7 fusion.50
  193.8 0.7 copy-done.13
  194.4 1.5 convolution_convert_fusion.2
  196.2 2.1 fusion.35
  198.3 1.1 copy.49
  199.4 1.3 multiply_reduce_fusion
  202.0 3.0 convolution_convert_fusion.1
  205.1 1.0 copy-done.8
  206.1 3.7 convolution_convert_fusion
  209.8 1.1 copy-done.9
  211.0 1.0 copy.60
  211.9 4.3 %all-to-all-start = ((bf16[128,8,384]{2,0,1:T(8,128)(2,1)}), bf16[128,8,384]{2,0,1:T(8,128)(2,1)}, u32[]{:S(2)}, u32[]{:S(2)}) async-start(bf16[128,8,384]{2,0,1:T(8,128)(2,1)} %bitcast.133), calls=%async_computation.3 | async-start | bytes 1572864 | tf_op jit(solution)/shard_map/all_to_all | solution.py:251
  217.9 1.7 convert_reduce_fusion
  219.6 0.6 convert_bitcast_fusion
  220.4 0.6 fusion.53
  221.1 4.8 %multiply_reduce_fusion.2 = (bf16[768]{0:T(1024)(128)(2,1)}, f32[128]{0:T(128)}, bf16[768]{0:T(1024)(128)(2,1)}, f32[128,768]{1,0:T(8,128)}) fusion(f32[128,768]{1,0:T(8,128)S(1)} %copy-done, f32[128]{0:T(128)} %copy-done.31, f32[128]{0:T(128)S(1)} %copy-done.28, f32[768]{0:T(1024)S(1)} %convert_element_type.288, ...), kind=kOutput, calls=%fused_computation.57 | convolution fusion | flops 455539072 | bytes 4922880 | tf_op jit(solution)/shard_map/dot_general | solution.py:40
  225.9 35.2 %all-reduce.16 = (bf16[768]{0:T(1024)(128)(2,1)S(1)}, bf16[768]{0:T(1024)(128)(2,1)S(1)}, bf16[768]{0:T(1024)(128)(2,1)S(1)}, bf16[768]{0:T(1024)(128)(2,1)S(1)}...) all-reduce(bf16[768]{0:T(1024)(128)(2,1)} %copy-done.38, ...), channel_id=14, replica_groups=mesh['rep'=4,'shard'=8] {'shard'}, use_global_device_ids=true, to_apply=%add.7 | all-reduce | flops 9216 | bytes 36864
  261.2 2.8 fusion.24
  264.0 32.5 %reduce-scatter.4.cloned.1.call-done = bf16[96,2304]{1,0:T(8,128)(2,1)} async-done(((bf16[768,2304]{1,0:T(8,128)(2,1)}), bf16[96,2304]{1,0:T(8,128)(2,1)}) %reduce-scatter.4.cloned.1.call-update) | async-done | bytes 442384 | tf_op jit(solution)/shard_map/reduce_scatter | solution.py:76
  296.5 55.8 %reduce-scatter.8.cloned.1.call-done = bf16[96,3072]{1,0:T(8,128)(2,1)} async-done(((bf16[768,3072]{1,0:T(8,128)(2,1)}), bf16[96,3072]{1,0:T(8,128)(2,1)}) %reduce-scatter.8.cloned.1.call-update) | async-done | bytes 589840 | tf_op jit(solution)/shard_map/reduce_scatter | solution.py:97
  352.6 10.1 %all-reduce.18 = (bf16[1,96]{1,0:T(2,128)(2,1)S(1)}, bf16[1,96]{1,0:T(2,128)(2,1)S(1)}, bf16[1,96]{1,0:T(2,128)(2,1)S(1)}, bf16[1,96]{1,0:T(2,128)(2,1)S(1)}, bf...) all-reduce(bf16[1,96]{1,0:T(2,128)(2,1)S(1)} %dynamic-slice_bitcast, ...), channel_id=1, replica_groups=mesh['rep'=4,'shard'=8] {'rep'}, use_global_device_ids=true, to_apply=%region_13.14 | all-reduce | flops 1152 | bytes 4608 | tf_op jit(solution)/shard_map/psum | solution.py:105
  362.7 0.5 stack.79
  365.3 0.5 stack.93
  366.3 0.6 stack.99
  366.9 0.5 stack.103
  367.7 0.9 add_add_fusion.2
  368.6 3.9 fusion.29
  372.5 46.5 %all-reduce.22.cloned.1.call-done = (bf16[1,96,2304]{2,1,0:T(8,128)(2,1)}, bf16[1,96,768]{2,1,0:T(8,128)(2,1)}, bf16[1,96,3072]{2,1,0:T(8,128)(2,1)}, bf16[1,384,768]{2,1,0:T(8,128)(2,1)}) async-done(((bf16[1,96,2304]{2,1,0:T(8,128)(2,1)}, bf16[1,96,768]{2,1,0:T(8,128)(2,1)}, bf16[1,96,3072]{2,1,0:T(8,128)(2,1)}, bf16[1,384,768]{2,1,0:T(8,128)(2,1)}), (bf16[1,96,2304]{2,1,0:T(8,128)(2,1)}, ...) | async-done | bytes 1769488 | tf_op jit(solution)/shard_map/psum | solution.py:107
  419.0 2.1 stack.83
  421.1 1.6 stack.89
  422.7 1.1 stack.97
  423.8 1.1 stack.101
  (200 shorter events, 9.8 us)
Async XLA Ops:
  7.2 2.2 copy-start.21
  7.2 3.0 copy-start.15
  7.2 54.6 %all-gather.21.cloned.1.call-start = ((), (), s32[]{:S(2)}) async-start(), calls=%async_computation.8 | async-start | bytes 3981312 | tf_op jit(solution)/shard_map/all_gather | solution.py:54
  9.4 69.5 %all-gather.23.cloned.1.call-start = ((), (), s32[]{:S(2)}) async-start(), calls=%async_computation.9 | async-start | bytes 1327104 | tf_op jit(solution)/shard_map/all_gather | solution.py:57
  10.1 121.9 %all-gather.25.cloned.1.call-start = ((), (), s32[]{:S(2)}) async-start(), calls=%async_computation.10 | async-start | bytes 5308416 | tf_op jit(solution)/shard_map/all_gather | solution.py:61
  11.1 1.9 copy-start.50
  11.1 2.0 copy-start.51
  11.2 2.0 copy-start.52
  11.2 2.0 copy-start.53
  11.2 2.0 copy-start.42
  11.2 37.2 %copy-start = (f32[128,768]{1,0:T(8,128)S(1)}, f32[128,768]{1,0:T(8,128)}, u32[]{:S(2)}) copy-start(f32[128,768]{1,0:T(8,128)} %param.16) | copy-start | bytes 1179652
  11.2 172.9 %all-gather.27.cloned.1.call-start = ((), (), s32[]{:S(2)}) async-start(), calls=%async_computation.11 | async-start | bytes 5308416 | tf_op jit(solution)/shard_map/all_gather | solution.py:63
  12.1 36.7 %copy-start.41 = (s32[1,128]{1,0:T(1,128)S(1)}, s32[1,128]{1,0:T(1,128)}, u32[]{:S(2)}) copy-start(s32[1,128]{1,0:T(1,128)} %param.17) | copy-start | bytes 1540
  12.1 36.8 %copy-start.43 = (f32[1,384]{1,0:T(1,128)S(1)}, f32[1,384]{1,0:T(1,128)}, u32[]{:S(2)}) copy-start(f32[1,384]{1,0:T(1,128)} %param.29) | copy-start | bytes 4612
  12.2 205.7 %all-gather.19.cloned.1.call-start = ((), (), s32[]{:S(2)}) async-start(), calls=%async_computation.7 | async-start | bytes 1769472 | tf_op jit(solution)/shard_map/all_gather | solution.py:252
  12.9 251.1 %reduce-scatter.6.cloned.1.call-start = ((), (), s32[]{:S(2)}) async-start(), calls=%async_computation.5 | async-start | bytes 1327104 | tf_op jit(solution)/shard_map/reduce_scatter | solution.py:85
  48.4 13.4 %copy-start.22 = (f32[768]{0:T(1024)}, f32[768]{0:T(1024)S(1)}, u32[]{:S(2)}) copy-start(f32[768]{0:T(1024)S(1)} %convert_element_type.289) | copy-start | bytes 9220
  48.6 16.0 %copy-start.26 = (f32[128]{0:T(128)}, f32[128]{0:T(128)S(1)}, u32[]{:S(2)}) copy-start(f32[128]{0:T(128)S(1)} %broadcast_multiply_fusion.1) | copy-start | bytes 1540
  48.8 15.8 %copy-start.44 = (f32[128]{0:T(128)}, f32[128]{0:T(128)S(1)}, u32[]{:S(2)}) copy-start(f32[128]{0:T(128)S(1)} %multiply_reduce_fusion.6) | copy-start | bytes 1540
  48.8 15.8 %copy-start.31 = (f32[128]{0:T(128)}, f32[128]{0:T(128)S(1)}, u32[]{:S(2)}) copy-start(f32[128]{0:T(128)S(1)} %fusion.46) | copy-start | bytes 1540
  61.7 70.3 %copy-start.24 = (f32[768]{0:T(1024)}, f32[768]{0:T(1024)S(1)}, u32[]{:S(2)}) copy-start(f32[768]{0:T(1024)S(1)} %convert_element_type.292) | copy-start | bytes 9220
  65.7 71.4 %copy-start.11 = (bf16[12,64,128]{2,1,0:T(8,128)(2,1)}, bf16[12,64,128]{2,1,0:T(8,128)(2,1)S(1)}, u32[]{:S(2)}) copy-start(bf16[12,64,128]{2,1,0:T(8,128)(2,1)S(1)} %convolution_convert_fusion.5) | copy-start | bytes 589828
  80.6 111.7 %copy-start.29 = (f32[128]{0:T(128)}, f32[128]{0:T(128)S(1)}, u32[]{:S(2)}) copy-start(f32[128]{0:T(128)S(1)} %broadcast_multiply_fusion) | copy-start | bytes 1540
  80.8 111.5 %copy-start.34 = (f32[128]{0:T(128)}, f32[128]{0:T(128)S(1)}, u32[]{:S(2)}) copy-start(f32[128]{0:T(128)S(1)} %fusion.47) | copy-start | bytes 1540
  132.0 52.1 %copy-start.17 = (bf16[128,768]{1,0:T(8,128)(2,1)S(1)}, bf16[128,768]{1,0:T(8,128)(2,1)}, u32[]{:S(2)}) copy-start(bf16[128,768]{1,0:T(8,128)(2,1)} %convert_element_type.265) | copy-start | bytes 589828
  184.1 5.9 %copy-start.3 = (bf16[1,768,3072]{2,1,0:T(8,128)(2,1)S(1)}, bf16[1,768,3072]{2,1,0:T(8,128)(2,1)}, u32[]{:S(2)}) copy-start(bf16[1,768,3072]{2,1,0:T(8,128)(2,1)} %all-gather.25.cloned.1.call-done) | copy-start | bytes 14155780
  190.0 2.3 copy-start.7
  192.3 2.1 copy-start.12
  193.8 2.4 copy-start.2
  195.9 100.6 %reduce-scatter.4.cloned.1.call-start = ((), (), s32[]{:S(2)}) async-start(), calls=%async_computation.4 | async-start | bytes 3981312 | tf_op jit(solution)/shard_map/reduce_scatter | solution.py:76
  201.6 18.6 %copy-start.14 = (bf16[12,64,128]{2,1,0:T(8,128)(2,1)}, bf16[12,64,128]{2,1,0:T(8,128)(2,1)S(1)}, u32[]{:S(2)}) copy-start(bf16[12,64,128]{2,1,0:T(8,128)(2,1)S(1)} %fusion.38) | copy-start | bytes 589828
  205.0 147.3 %reduce-scatter.8.cloned.1.call-start = ((), (), s32[]{:S(2)}) async-start(), calls=%async_computation.6 | async-start | bytes 5308416 | tf_op jit(solution)/shard_map/reduce_scatter | solution.py:97
  210.9 6.7 %copy-start.54 = (f32[1,96]{1,0:T(1,128)S(1)}, f32[1,96]{1,0:T(1,128)}, u32[]{:S(2)}) copy-start(f32[1,96]{1,0:T(1,128)} %param.31) | copy-start | bytes 1156
  211.9 9.1 %copy-start.28 = (f32[128]{0:T(128)S(1)}, f32[128]{0:T(128)}, u32[]{:S(2)}) copy-start(f32[128]{0:T(128)} %copy-done.26) | copy-start | bytes 1540
  211.9 49.3 %all-to-all-start = ((bf16[128,8,384]{2,0,1:T(8,128)(2,1)}), bf16[128,8,384]{2,0,1:T(8,128)(2,1)}, u32[]{:S(2)}, u32[]{:S(2)}) async-start(bf16[128,8,384]{2,0,1:T(8,128)(2,1)} %bitcast.133), calls=%async_computation.3 | async-start | bytes 1572864 | tf_op jit(solution)/shard_map/all_to_all | solution.py:251
  216.3 202.7 %all-reduce.22.cloned.1.call-start = ((), (), s32[]{:S(2)}) async-start(), calls=%async_computation.12 | async-start | bytes 3538944 | tf_op jit(solution)/shard_map/psum | solution.py:107
  221.1 4.8 %copy-start.36 = (bf16[768]{0:T(1024)(128)(2,1)S(1)}, bf16[768]{0:T(1024)(128)(2,1)}, u32[]{:S(2)}) copy-start(bf16[768]{0:T(1024)(128)(2,1)} %get-tuple-element.56) | copy-start | bytes 4612
  221.1 4.8 %copy-start.37 = (bf16[768]{0:T(1024)(128)(2,1)S(1)}, bf16[768]{0:T(1024)(128)(2,1)}, u32[]{:S(2)}) copy-start(bf16[768]{0:T(1024)(128)(2,1)} %get-tuple-element.70) | copy-start | bytes 4612
  221.1 40.1 %copy-start.1 = (bf16[1024,768]{1,0:T(8,128)(2,1)S(1)}, bf16[1024,768]{1,0:T(8,128)(2,1)}, u32[]{:S(2)}) copy-start(bf16[1024,768]{1,0:T(8,128)(2,1)} %all-gather.19.cloned.1.call-done) | copy-start | bytes 4718596
  264.0 88.7 %copy-start.46 = (bf16[1,96]{1,0:T(2,128)(2,1)S(1)}, bf16[1,96]{1,0:T(2,128)(2,1)}, u32[]{:S(2)}) copy-start(bf16[1,96]{1,0:T(2,128)(2,1)} %convert_bitcast_fusion) | copy-start | bytes 580
  264.0 103.4 %copy-start.45 = (f32[128]{0:T(128)S(1)}, f32[128]{0:T(128)}, u32[]{:S(2)}) copy-start(f32[128]{0:T(128)} %copy-done.44) | copy-start | bytes 1540
  264.0 103.4 %copy-start.55 = (f32[128]{0:T(128)S(1)}, f32[128]{0:T(128)}, u32[]{:S(2)}) copy-start(f32[128]{0:T(128)} %get-tuple-element.69) | copy-start | bytes 1540
  264.0 103.5 %copy-start.20 = (f32[128,768]{1,0:T(8,128)S(1)}, f32[128,768]{1,0:T(8,128)}, u32[]{:S(2)}) copy-start(f32[128,768]{1,0:T(8,128)} %get-tuple-element.120) | copy-start | bytes 1179652
  264.0 103.5 %copy-start.33 = (f32[128]{0:T(128)S(1)}, f32[128]{0:T(128)}, u32[]{:S(2)}) copy-start(f32[128]{0:T(128)} %copy-done.31) | copy-start | bytes 1540
  264.0 103.7 %copy-start.40 = (f32[128]{0:T(128)S(1)}, f32[128]{0:T(128)}, u32[]{:S(2)}) copy-start(f32[128]{0:T(128)} %copy-done.39) | copy-start | bytes 1540
  352.3 16.3 %copy-start.10 = (bf16[128,3072]{1,0:T(8,128)(2,1)S(1)}, bf16[128,3072]{1,0:T(8,128)(2,1)}, u32[]{:S(2)}) copy-start(bf16[128,3072]{1,0:T(8,128)(2,1)} %get-tuple-element.115) | copy-start | bytes 2359300
  419.0 3.7 copy-start.19
  419.0 4.8 %copy-start.18 = (bf16[1,384,768]{2,1,0:T(8,128)(2,1)S(1)}, bf16[1,384,768]{2,1,0:T(8,128)(2,1)}, u32[]{:S(2)}) copy-start(bf16[1,384,768]{2,1,0:T(8,128)(2,1)} %get-tuple-element.100) | copy-start | bytes 1769476
  (18 other events, 22.9 us)
Sparse Core Ops, SparseCore 0:
  10.2 44.7 all-gather.20
  57.2 21.6 all-gather.22
  81.1 50.8 all-gather.24
  134.1 49.9 all-gather.26
  186.1 24.0 all-gather.18
  212.9 36.2 reduce-scatter.5
  251.5 44.9 reduce-scatter.3
  298.8 53.4 reduce-scatter.7
  356.3 62.6 all-reduce.21
where the time goes:
time: 432 us; the launch traced here: 431 us
  waiting for transfers between devices  246 us (57%)
  blocking collectives  90.6 us (21%)
  matrix products  42.4 us (10%)
  other arithmetic  20.8 us (5%)
  between operations  16.6 us (4%)
  local copies, waits for them, and re-layouts  9.89 us (2%)
  starting transfers between devices  4.9 us (1%)
    reduce_scatter x1, waiting for transfers between devices, reduce_nested_rest(): lax.psum_scatter(grads[9].astype(jnp.bfloat16), 'shard', scatter_dimensio...  55.8 us
    all_gather x1, waiting for transfers between devices, fetch_forward(): lax.all_gather(parts[9], 'shard', axis=0, tiled=True)  51.2 us
    all_gather x1, waiting for transfers between devices, fetch_forward(): lax.all_gather(parts[11], 'shard', axis=0, tiled=True)  47 us
    psum x1, waiting for transfers between devices, reduce_nested_rest(): lax.psum(owned[2].astype(jnp.bfloat16), 'rep').astype(jnp.float32)  46.5 us
    unnamed x1, blocking collectives  35.2 us
    all_gather x1, blocking collectives, fetch_forward(): lax.all_gather(parts[4], 'shard', axis=0, tiled=True)  32.5 us
    reduce_scatter x1, waiting for transfers between devices, reduce_nested_rest(): lax.psum_scatter(grads[2].astype(jnp.bfloat16), 'shard', scatter_dimensio...  32.5 us
    dot_general x4, matrix products, project_trans(): lax.dot_general(left, right, (((1,), (1,)), ((), ())), preferred_element_...  15.2 us
  transfers between devices with their start and end apart: 10, of which 6 were waited for; matrix products, arithmetic and copies ran while one was open for 14% of the time, Pallas kernels for 0%

commit v1 on v0

--- a/solution.py
+++ b/solution.py
@@ -2,6 +2,7 @@
 import jax.numpy as jnp
 from jax import lax
 from jax.sharding import PartitionSpec as P
+from jax.lax import axis_index, axis_size, ppermute
 
 HEADS = 12
 HEAD = 64
@@ -11,6 +12,12 @@
 NEG_FILL = -1e30
 
 
+def guide_limits(message, array_dim):
+    y = list(message.shape[1:])
+    y[array_dim] *= message.shape[0]
+    return jnp.moveaxis(message, 0, array_dim).reshape(y)
+
+
 def norm(values_in, gains, shifts):
     average = jnp.mean(values_in, axis=-1, keepdims=True)
     centred = values_in - average
@@ -48,6 +55,26 @@
 
 def fetch_forward(shards, layer_index):
     parts = layer_slices(shards, layer_index)
+
+    def work_the_surface(in_dim, mine_x, row_axis):
+        n_slots = axis_size(row_axis)
+        pool = [(rr, (rr + 1) % n_slots) for rr in range(n_slots)]
+        inbox = [(h, dd) for dd, h in pool]
+        local_part, w1 = ([], [])
+        for j0 in [*range(n_slots - 1)]:
+            if j0 % 2 == 0:
+                local_part.append(
+                    ppermute(
+                        local_part[-1] if local_part else mine_x, perm=pool, axis_name=row_axis
+                    )
+                )
+            else:
+                w1.append(ppermute(w1[-1] if w1 else mine_x, axis_name=row_axis, perm=inbox))
+        all_rows = jnp.stack([*local_part[::-1], mine_x, *w1])
+        mixed_arr = axis_index(row_axis) - len(local_part)
+        all_rows = all_rows[(jnp.arange(n_slots) - mixed_arr) % n_slots]
+        return guide_limits(all_rows, in_dim)
+
     return (
         lax.all_gather(parts[0], "shard", axis=0, tiled=True),
         lax.all_gather(parts[1], "shard", axis=0, tiled=True),
@@ -60,7 +87,7 @@
         lax.all_gather(parts[8], "shard", axis=0, tiled=True),
         lax.all_gather(parts[9], "shard", axis=0, tiled=True),
         lax.all_gather(parts[10], "shard", axis=0, tiled=True),
-        lax.all_gather(parts[11], "shard", axis=0, tiled=True),
+        work_the_surface(0, parts[11], "shard"),
         lax.all_gather(parts[12], "shard", axis=0, tiled=True),
     )
 

time: 432 us -> 404 us (0.935)
  waiting for transfers between devices: 246 us -> 177 us
  local copies, waits for them, and re-layouts: 9.89 us -> 26.8 us
  blocking collectives: 90.6 us -> 106 us
  starting transfers between devices: 4.9 us -> 17.8 us
    all_gather x1 -> x0, waiting for transfers between devices: 47 us -> none  [fetch_forward(): lax.all_gather(parts[11], 'shard', axis=0, tiled=True)]
    ppermute x0 -> x7, waiting for transfers between devices: none -> 44.9 us  [the longest x4 34 us: work_the_surface(): ppermute(local_part[-1] if local_part else mine_x, perm=pool, axis_name=r...]
    all_gather x1, waiting for transfers between devices: 51.2 us -> 6.93 us  [fetch_forward(): lax.all_gather(parts[9], 'shard', axis=0, tiled=True)]
    all_gather x1, waiting for transfers between devices: 13.2 us -> 0.01 us  [fetch_forward(): lax.all_gather(parts[5], 'shard', axis=0, tiled=True)]
    unnamed x131 -> x143, local copies, waits for them, and re-layouts: 6.02 us -> 14.9 us
    ppermute x0 -> x7, starting transfers between devices: none -> 8.71 us  [the longest x3 7.03 us: work_the_surface(): ppermute(w1[-1] if w1 else mine_x, axis_name=row_axis, perm=inbox)]
    all_gather x1, blocking collectives: 12.8 us -> 20.4 us  [fetch_forward(): lax.all_gather(parts[10], 'shard', axis=0, tiled=True)]
    reduce_scatter x1, waiting for transfers between devices: 32.5 us -> 26 us  [reduce_nested_rest(): lax.psum_scatter(grads[2].astype(jnp.bfloat16), 'shard', scatter_dimensio...]
  transfers between devices with their start and end apart: 10 -> 16, of which waited for: 6 -> 7; matrix products, arithmetic and copies ran while one was open for 14% -> 19% of each run, Pallas kernels for 0% -> 0%
where the time goes in v1:
time: 404 us; the launch traced here: 403 us
  waiting for transfers between devices  177 us (44%)
  blocking collectives  106 us (26%)
  matrix products  39.1 us (10%)
  local copies, waits for them, and re-layouts  26.8 us (7%)
  other arithmetic  20 us (5%)
  starting transfers between devices  17.8 us (4%)
  between operations  16.9 us (4%)
    reduce_scatter x1, waiting for transfers between devices, reduce_nested_rest(): lax.psum_scatter(grads[9].astype(jnp.bfloat16), 'shard', scatter_dimensio...  55.7 us
    psum x1, waiting for transfers between devices, reduce_nested_rest(): lax.psum(owned[2].astype(jnp.bfloat16), 'rep').astype(jnp.float32)  43.2 us
    all_gather x1, blocking collectives, fetch_forward(): lax.all_gather(parts[4], 'shard', axis=0, tiled=True)  38.1 us
    unnamed x1, blocking collectives  36.7 us
    ppermute x4, waiting for transfers between devices, work_the_surface(): ppermute(local_part[-1] if local_part else mine_x, perm=pool, axis_name=r...  34 us
    reduce_scatter x1, waiting for transfers between devices, reduce_nested_rest(): lax.psum_scatter(grads[2].astype(jnp.bfloat16), 'shard', scatter_dimensio...  26 us
    all_gather x1, blocking collectives, fetch_forward(): lax.all_gather(parts[10], 'shard', axis=0, tiled=True)  20.4 us
    unnamed x143, local copies, waits for them, and re-layouts  14.9 us
  transfers between devices with their start and end apart: 16, of which 7 were waited for; matrix products, arithmetic and copies ran while one was open for 19% of the time, Pallas kernels for 0%

profile of v1, /device:TPU:0, one launch (start us, length us, event | category | flops | bytes accessed | tf_op | source)
XLA Modules:
  0.0 403.3 jit_solution(17041717350738038368)
XLA Ops:
  7.2 2.1 convert_element_type.232
  10.2 0.9 convert_element_type.255
  11.9 4.1 %collective-permute-start.4 = (bf16[384,768]{1,0:T(8,128)(2,1)S(1)}, bf16[384,768]{1,0:T(8,128)(2,1)S(1)}, u32[]{:S(2)}, u32[]{:S(2)}) collective-permute-start(bf16[384,768]{1,0:T(8,128)(2,1)S(1)} %convert_bitcast_fusion), channel_id=1, source_target_pairs={{1,0},{2,1},{3,2},{4,3},{5,4},{6,5},{7,6},{0,7},{9,8},{10,9},{11,1... | collective-permute-start | bytes 1769480 | tf_op jit(solution)/shard_map/ppermute | solution.py:72
  18.8 10.5 %collective-permute-done = bf16[384,768]{1,0:T(8,128)(2,1)} collective-permute-done((bf16[384,768]{1,0:T(8,128)(2,1)S(1)}, bf16[384,768]{1,0:T(8,128)(2,1)}, u32[]{:S(2)}, u32[]{:S(2)}) %collective-permute-start) | collective-permute-done | bytes 589856 | tf_op jit(solution)/shard_map/ppermute | solution.py:67
  30.6 23.6 %collective-permute-done.1 = bf16[384,768]{1,0:T(8,128)(2,1)} collective-permute-done((bf16[384,768]{1,0:T(8,128)(2,1)}, bf16[384,768]{1,0:T(8,128)(2,1)}, u32[]{:S(2)}, u32[]{:S(2)}) %collective-permute-start.1) | collective-permute-done | bytes 589856 | tf_op jit(solution)/shard_map/ppermute | solution.py:67
  54.5 38.1 %all-reduce.17 = (bf16[768]{0:T(1024)(128)(2,1)S(1)}, bf16[768]{0:T(1024)(128)(2,1)S(1)}, bf16[768]{0:T(1024)(128)(2,1)S(1)}, bf16[768]{0:T(1024)(128)(2,1)S(1)}...) all-reduce(bf16[768]{0:T(1024)(128)(2,1)S(1)} %dynamic-update-slice, ...), channel_id=6, replica_groups=mesh['rep'=4,'shard'=8] {'shard'}, use_global_device_ids=true, to_apply=%add.3 | all-reduce | flops 5376 | bytes 21504 | tf_op jit(solution)/shard_map/all_gather | solution.py:83
  93.4 20.4 %all-gather.10 = bf16[1,3072]{1,0:T(2,128)(2,1)S(1)} all-gather(bf16[1,384]{1,0:T(2,128)(2,1)S(1)} %convert_element_type.257), channel_id=12, replica_groups=mesh['rep'=4,'shard'=8] {'shard'}, dimensions={1}, use_global_device_ids=true | all-gather | bytes 6912 | tf_op jit(solution)/shard_map/all_gather | solution.py:89
  114.1 2.9 collective-permute-start.6
  117.0 0.8 bitcast_dynamic-update-slice_fusion.6
  117.9 1.9 bitcast_dynamic-update-slice_fusion.5
  119.8 1.9 bitcast_dynamic-update-slice_fusion.4
  121.7 1.9 bitcast_dynamic-update-slice_fusion.3
  123.7 0.9 convert_dynamic-update-slice_fusion
  124.5 0.9 bitcast_dynamic-update-slice_fusion.2
  125.5 0.8 bitcast_dynamic-update-slice_fusion.1
  126.3 10.9 %collective-permute-done.6 = bf16[384,768]{1,0:T(8,128)(2,1)S(1)} collective-permute-done((bf16[384,768]{1,0:T(8,128)(2,1)S(1)}, bf16[384,768]{1,0:T(8,128)(2,1)S(1)}, u32[]{:S(2)}, u32[]{:S(2)}) %collective-permute-start.6) | collective-permute-done | bytes 589856 | tf_op jit(solution)/shard_map/ppermute | solution.py:72
  137.2 0.8 bitcast_dynamic-update-slice_fusion
  138.0 5.3 %gather_fusion = bf16[8,384,768]{2,1,0:T(8,128)(2,1)} fusion(bf16[8,384,768]{2,1,0:T(8,128)(2,1)} %bitcast_dynamic-update-slice_fusion, s32[1024]{0:T(1024)S(1)} %pad_clamp_fusion), kind=kCustom, calls=%fused_computation | custom fusion | bytes 9437216 | tf_op jit(solution)/shard_map/gather | solution.py:75
  143.4 2.7 fusion.7
  147.2 1.7 fusion.47
  149.1 6.9 %all-gather.23.cloned.1.call-done = bf16[1,768,3072]{2,1,0:T(8,128)(2,1)} async-done(((bf16[1,96,3072]{2,1,0:T(8,128)(2,1)}), bf16[1,768,3072]{2,1,0:T(8,128)(2,1)}) %all-gather.23.cloned.1.call-update) | async-done | bytes 4718608 | tf_op jit(solution)/shard_map/all_gather | solution.py:88
  156.1 4.7 %multiply_convert_fusion = (bf16[128,3072]{1,0:T(8,128)(2,1)}, f32[128,3072]{1,0:T(8,128)S(1)}) fusion(f32[3072]{0:T(1024)S(1)} %bitcast.173, bf16[1,768,3072]{2,1,0:T(8,128)(2,1)} %all-gather.23.cloned.1.call-done, f32[128,768]{1,0:T(8,128)S(1)} %get-tuple-element.114, f32[768]{0:T(1024)S(1)} %convert_element_type.293, f32[768]{0:T(1024)S(1)} %convert_element_type.292, ...), kind=kOutput, calls=%fused_computation.25 | convolution fusion | flops 608403456 | bytes 7490560 | tf_op jit(solution)/shard_map/dot_general | solution.py:37
  160.8 5.4 %fusion.48 = (bf16[3072]{0:T(1024)(128)(2,1)}, bf16[128,3072]{1,0:T(8,128)(2,1)S(1)}) fusion(f32[128,3072]{1,0:T(8,128)S(1)} %get-tuple-element.116, bf16[3072,768]{1,0:T(8,128)(2,1)} %bitcast.146, bf16[128,768]{1,0:T(8,128)(2,1)S(1)} %copy-done.17), kind=kOutput, calls=%fused_computation.123 | convolution fusion | flops 613807104 | bytes 7280640 | tf_op jit(solution)/shard_map/dot_general | solution.py:47
  166.2 2.3 multiply_reduce_fusion.1
  170.2 1.5 convolution_convert_fusion.2
  172.7 1.3 multiply_reduce_fusion
  175.3 3.1 convolution_convert_fusion.1
  178.5 1.1 copy-done.10
  179.5 3.7 convolution_convert_fusion
  183.3 1.1 copy-done.11
  184.4 1.0 copy.60
  185.4 8.6 %all-to-all-start = ((bf16[128,8,384]{2,0,1:T(8,128)(2,1)}), bf16[128,8,384]{2,0,1:T(8,128)(2,1)S(1)}, u32[]{:S(2)}, u32[]{:S(2)}) async-start(bf16[128,8,384]{2,0,1:T(8,128)(2,1)} %bitcast.145), calls=%async_computation.3 | async-start | bytes 1572864 | tf_op jit(solution)/shard_map/all_to_all | solution.py:278
  195.6 1.7 convert_reduce_fusion
  198.8 5.1 %multiply_reduce_fusion.2 = (bf16[768]{0:T(1024)(128)(2,1)}, f32[128]{0:T(128)}, bf16[768]{0:T(1024)(128)(2,1)}, f32[128,768]{1,0:T(8,128)}) fusion(f32[128,768]{1,0:T(8,128)S(1)} %copy-done, f32[128]{0:T(128)S(1)} %copy-done.34, f32[128]{0:T(128)S(1)} %copy-done.29, f32[768]{0:T(1024)S(1)} %convert_element_type.289, ...), kind=kOutput, calls=%fused_computation.62 | convolution fusion | flops 455539072 | bytes 4922880 | tf_op jit(solution)/shard_map/dot_general | solution.py:47
  203.8 36.7 %all-reduce.16 = (bf16[768]{0:T(1024)(128)(2,1)}, bf16[768]{0:T(1024)(128)(2,1)}, bf16[768]{0:T(1024)(128)(2,1)}, bf16[768]{0:T(1024)(128)(2,1)}, bf16[768]{0:T(...) all-reduce(bf16[768]{0:T(1024)(128)(2,1)} %copy-done.38, ...), channel_id=13, replica_groups=mesh['rep'=4,'shard'=8] {'shard'}, use_global_device_ids=true, to_apply=%add.7 | all-reduce | flops 9216 | bytes 36864
  240.5 0.8 dynamic-slice.24
  241.3 1.6 fusion.18
  243.0 26.0 %reduce-scatter.4.cloned.1.call-done = bf16[96,2304]{1,0:T(8,128)(2,1)} async-done(((bf16[768,2304]{1,0:T(8,128)(2,1)}), bf16[96,2304]{1,0:T(8,128)(2,1)}) %reduce-scatter.4.cloned.1.call-update) | async-done | bytes 442384 | tf_op jit(solution)/shard_map/reduce_scatter | solution.py:103
  269.0 55.7 %reduce-scatter.8.cloned.1.call-done = bf16[96,3072]{1,0:T(8,128)(2,1)} async-done(((bf16[768,3072]{1,0:T(8,128)(2,1)}), bf16[96,3072]{1,0:T(8,128)(2,1)}) %reduce-scatter.8.cloned.1.call-update) | async-done | bytes 589840 | tf_op jit(solution)/shard_map/reduce_scatter | solution.py:124
  324.8 0.8 dynamic-slice_bitcast_fusion.6
  327.1 0.8 dynamic-slice_bitcast_fusion.4
  327.9 10.5 %all-reduce.18 = (bf16[1,96]{1,0:T(2,128)(2,1)S(1)}, bf16[1,96]{1,0:T(2,128)(2,1)S(1)}, bf16[1,96]{1,0:T(2,128)(2,1)S(1)}, bf16[1,96]{1,0:T(2,128)(2,1)S(1)}, bf...) all-reduce(bf16[1,96]{1,0:T(2,128)(2,1)S(1)} %dynamic-slice_bitcast, ...), channel_id=1, replica_groups=mesh['rep'=4,'shard'=8] {'rep'}, use_global_device_ids=true, to_apply=%region_13.14 | all-reduce | flops 1152 | bytes 4608 | tf_op jit(solution)/shard_map/psum | solution.py:132
  343.3 0.9 add_add_fusion.2
  344.2 4.0 fusion.20
  348.2 43.2 %all-reduce.22.cloned.1.call-done = (bf16[1,96,2304]{2,1,0:T(8,128)(2,1)}, bf16[1,96,768]{2,1,0:T(8,128)(2,1)}, bf16[1,96,3072]{2,1,0:T(8,128)(2,1)}, bf16[1,384,768]{2,1,0:T(8,128)(2,1)}) async-done(((bf16[1,96,2304]{2,1,0:T(8,128)(2,1)}, bf16[1,96,768]{2,1,0:T(8,128)(2,1)}, bf16[1,96,3072]{2,1,0:T(8,128)(2,1)}, bf16[1,384,768]{2,1,0:T(8,128)(2,1)}), (bf16[1,96,2304]{2,1,0:T(8,128)(2,1)}, ...) | async-done | bytes 1769488 | tf_op jit(solution)/shard_map/psum | solution.py:134
  391.4 2.3 stack.130
  393.7 1.1 stack.134
  394.8 1.0 stack.116
  (229 shorter events, 20.5 us)
Async XLA Ops:
  7.2 136.2 %all-gather.19.cloned.1.call-start = ((), (), s32[]{:S(2)}) async-start(), calls=%async_computation.8 | async-start | bytes 3981312 | tf_op jit(solution)/shard_map/all_gather | solution.py:81
  9.4 137.8 %all-gather.21.cloned.1.call-start = ((), (), s32[]{:S(2)}) async-start(), calls=%async_computation.9 | async-start | bytes 1327104 | tf_op jit(solution)/shard_map/all_gather | solution.py:84
  10.1 146.0 %all-gather.23.cloned.1.call-start = ((), (), s32[]{:S(2)}) async-start(), calls=%async_computation.10 | async-start | bytes 5308416 | tf_op jit(solution)/shard_map/all_gather | solution.py:88
  11.1 7.2 %copy-start.49 = (f32[1,96]{1,0:T(1,128)S(1)}, f32[1,96]{1,0:T(1,128)}, u32[]{:S(2)}) copy-start(f32[1,96]{1,0:T(1,128)} %param.20) | copy-start | bytes 1156
  11.1 7.4 %copy-start.50 = (f32[1,96]{1,0:T(1,128)S(1)}, f32[1,96]{1,0:T(1,128)}, u32[]{:S(2)}) copy-start(f32[1,96]{1,0:T(1,128)} %param.22) | copy-start | bytes 1156
  11.1 18.8 %copy-start.51 = (f32[1,96]{1,0:T(1,128)S(1)}, f32[1,96]{1,0:T(1,128)}, u32[]{:S(2)}) copy-start(f32[1,96]{1,0:T(1,128)} %param.23) | copy-start | bytes 1156
  11.1 19.0 %copy-start.52 = (f32[1,96]{1,0:T(1,128)S(1)}, f32[1,96]{1,0:T(1,128)}, u32[]{:S(2)}) copy-start(f32[1,96]{1,0:T(1,128)} %param.25) | copy-start | bytes 1156
  11.1 19.2 %copy-start.53 = (f32[1,96]{1,0:T(1,128)S(1)}, f32[1,96]{1,0:T(1,128)}, u32[]{:S(2)}) copy-start(f32[1,96]{1,0:T(1,128)} %param.26) | copy-start | bytes 1156
  11.1 43.0 %copy-start.54 = (f32[1,96]{1,0:T(1,128)S(1)}, f32[1,96]{1,0:T(1,128)}, u32[]{:S(2)}) copy-start(f32[1,96]{1,0:T(1,128)} %param.27) | copy-start | bytes 1156
  11.1 43.3 %copy-start = (f32[128,768]{1,0:T(8,128)S(1)}, f32[128,768]{1,0:T(8,128)}, u32[]{:S(2)}) copy-start(f32[128,768]{1,0:T(8,128)} %param.16) | copy-start | bytes 1179652
  11.2 82.2 %copy-start.44 = (f32[1,384]{1,0:T(1,128)S(1)}, f32[1,384]{1,0:T(1,128)}, u32[]{:S(2)}) copy-start(f32[1,384]{1,0:T(1,128)} %param.29) | copy-start | bytes 4612
  11.2 102.8 %copy-start.42 = (s32[1,128]{1,0:T(1,128)S(1)}, s32[1,128]{1,0:T(1,128)}, u32[]{:S(2)}) copy-start(s32[1,128]{1,0:T(1,128)} %param.17) | copy-start | bytes 1540
  11.2 184.4 %all-gather.17.cloned.1.call-start = ((), (), s32[]{:S(2)}) async-start(), calls=%async_computation.7 | async-start | bytes 1769472 | tf_op jit(solution)/shard_map/all_gather | solution.py:279
  11.3 17.9 %collective-permute-start = (bf16[384,768]{1,0:T(8,128)(2,1)S(1)}, bf16[384,768]{1,0:T(8,128)(2,1)}, u32[]{:S(2)}, u32[]{:S(2)}) collective-permute-start(bf16[384,768]{1,0:T(8,128)(2,1)S(1)} %convert_bitcast_fusion), channel_id=1, source_target_pairs={{0,1},{1,2},{2,3},{3,4},{4,5},{5,6},{6,7},{7,0},{8,9},{9,10},{10,1... | collective-permute-start | bytes 1769480 | tf_op jit(solution)/shard_map/ppermute | solution.py:67
  11.9 80.8 %collective-permute-start.4 = (bf16[384,768]{1,0:T(8,128)(2,1)S(1)}, bf16[384,768]{1,0:T(8,128)(2,1)S(1)}, u32[]{:S(2)}, u32[]{:S(2)}) collective-permute-start(bf16[384,768]{1,0:T(8,128)(2,1)S(1)} %convert_bitcast_fusion), channel_id=1, source_target_pairs={{1,0},{2,1},{3,2},{4,3},{5,4},{6,5},{7,6},{0,7},{9,8},{10,9},{11,1... | collective-permute-start | bytes 1769480 | tf_op jit(solution)/shard_map/ppermute | solution.py:72
  16.7 226.3 %reduce-scatter.6.cloned.1.call-start = ((), (), s32[]{:S(2)}) async-start(), calls=%async_computation.5 | async-start | bytes 1327104 | tf_op jit(solution)/shard_map/reduce_scatter | solution.py:112
  29.2 24.9 %collective-permute-start.1 = (bf16[384,768]{1,0:T(8,128)(2,1)}, bf16[384,768]{1,0:T(8,128)(2,1)}, u32[]{:S(2)}, u32[]{:S(2)}) collective-permute-start(bf16[384,768]{1,0:T(8,128)(2,1)} %collective-permute-done), channel_id=1, source_target_pairs={{0,1},{1,2},{2,3},{3,4},{4,5},{5,6},{6,7},{7,0},{8,9},{9,10},{10,1... | collective-permute-start | bytes 1769480 | tf_op jit(solution)/shard_map/ppermute | solution.py:67
  54.2 38.6 %collective-permute-start.2 = (bf16[384,768]{1,0:T(8,128)(2,1)}, bf16[384,768]{1,0:T(8,128)(2,1)}, u32[]{:S(2)}, u32[]{:S(2)}) collective-permute-start(bf16[384,768]{1,0:T(8,128)(2,1)} %collective-permute-done.1), channel_id=1, source_target_pairs={{0,1},{1,2},{2,3},{3,4},{4,5},{5,6},{6,7},{7,0},{8,9},{9,10},{10,1... | collective-permute-start | bytes 1769480 | tf_op jit(solution)/shard_map/ppermute | solution.py:67
  92.7 50.7 %copy-start.27 = (f32[128]{0:T(128)}, f32[128]{0:T(128)S(1)}, u32[]{:S(2)}) copy-start(f32[128]{0:T(128)S(1)} %broadcast_multiply_fusion.1) | copy-start | bytes 1540
  92.7 21.4 %collective-permute-start.5 = (bf16[384,768]{1,0:T(8,128)(2,1)S(1)}, bf16[384,768]{1,0:T(8,128)(2,1)S(1)}, u32[]{:S(2)}, u32[]{:S(2)}) collective-permute-start(bf16[384,768]{1,0:T(8,128)(2,1)S(1)} %collective-permute-done.4), channel_id=1, source_target_pairs={{1,0},{2,1},{3,2},{4,3},{5,4},{6,5},{7,6},{0,7},{9,8},{10,9},{11,1... | collective-permute-start | bytes 1769480 | tf_op jit(solution)/shard_map/ppermute | solution.py:72
  92.8 24.3 %collective-permute-start.3 = (bf16[384,768]{1,0:T(8,128)(2,1)}, bf16[384,768]{1,0:T(8,128)(2,1)S(1)}, u32[]{:S(2)}, u32[]{:S(2)}) collective-permute-start(bf16[384,768]{1,0:T(8,128)(2,1)} %collective-permute-done.2), channel_id=1, source_target_pairs={{0,1},{1,2},{2,3},{3,4},{4,5},{5,6},{6,7},{7,0},{8,9},{9,10},{10,1... | collective-permute-start | bytes 1769480 | tf_op jit(solution)/shard_map/ppermute | solution.py:67
  93.3 50.1 %copy-start.23 = (f32[768]{0:T(1024)}, f32[768]{0:T(1024)S(1)}, u32[]{:S(2)}) copy-start(f32[768]{0:T(1024)S(1)} %convert_element_type.290) | copy-start | bytes 9220
  93.3 62.7 %copy-start.25 = (f32[768]{0:T(1024)}, f32[768]{0:T(1024)S(1)}, u32[]{:S(2)}) copy-start(f32[768]{0:T(1024)S(1)} %convert_element_type.293) | copy-start | bytes 9220
  114.0 7.7 %copy-start.45 = (f32[128]{0:T(128)}, f32[128]{0:T(128)S(1)}, u32[]{:S(2)}) copy-start(f32[128]{0:T(128)S(1)} %multiply_reduce_fusion.6) | copy-start | bytes 1540
  114.0 29.4 %copy-start.32 = (f32[128]{0:T(128)}, f32[128]{0:T(128)S(1)}, u32[]{:S(2)}) copy-start(f32[128]{0:T(128)S(1)} %fusion.37) | copy-start | bytes 1540
  114.1 23.0 %collective-permute-start.6 = (bf16[384,768]{1,0:T(8,128)(2,1)S(1)}, bf16[384,768]{1,0:T(8,128)(2,1)S(1)}, u32[]{:S(2)}, u32[]{:S(2)}) collective-permute-start(bf16[384,768]{1,0:T(8,128)(2,1)S(1)} %collective-permute-done.5), channel_id=1, source_target_pairs={{1,0},{2,1},{3,2},{4,3},{5,4},{6,5},{7,6},{0,7},{9,8},{10,9},{11,1... | collective-permute-start | bytes 1769480 | tf_op jit(solution)/shard_map/ppermute | solution.py:72
  148.9 19.6 %copy-start.30 = (f32[128]{0:T(128)}, f32[128]{0:T(128)S(1)}, u32[]{:S(2)}) copy-start(f32[128]{0:T(128)S(1)} %broadcast_multiply_fusion) | copy-start | bytes 1540
  149.1 19.4 %copy-start.35 = (f32[128]{0:T(128)}, f32[128]{0:T(128)S(1)}, u32[]{:S(2)}) copy-start(f32[128]{0:T(128)S(1)} %fusion.38) | copy-start | bytes 1540
  156.1 10.1 %slice-start = ((s8[4718592]{0:T(1024)(128)(4,1)}), s8[4194304]{0:T(1024)(128)(4,1)S(1)}, s32[]{:S(2)}) async-start(s8[4718592]{0:T(1024)(128)(4,1)} %bitcast.148), calls=%async_computation.12 | async-start | bytes 8388608
  171.7 97.3 %reduce-scatter.4.cloned.1.call-start = ((), (), s32[]{:S(2)}) async-start(), calls=%async_computation.4 | async-start | bytes 3981312 | tf_op jit(solution)/shard_map/reduce_scatter | solution.py:103
  174.5 23.4 %copy-start.14 = (bf16[12,64,128]{2,1,0:T(8,128)(2,1)}, bf16[12,64,128]{2,1,0:T(8,128)(2,1)S(1)}, u32[]{:S(2)}) copy-start(bf16[12,64,128]{2,1,0:T(8,128)(2,1)S(1)} %fusion.27) | copy-start | bytes 589828
  174.9 23.0 %copy-start.15 = (bf16[12,64,128]{2,1,0:T(8,128)(2,1)}, bf16[12,64,128]{2,1,0:T(8,128)(2,1)S(1)}, u32[]{:S(2)}) copy-start(bf16[12,64,128]{2,1,0:T(8,128)(2,1)S(1)} %fusion.28) | copy-start | bytes 589828
  175.2 22.6 %copy-start.13 = (bf16[12,64,128]{2,1,0:T(8,128)(2,1)}, bf16[12,64,128]{2,1,0:T(8,128)(2,1)S(1)}, u32[]{:S(2)}) copy-start(bf16[12,64,128]{2,1,0:T(8,128)(2,1)S(1)} %convolution_convert_fusion.4) | copy-start | bytes 589828
  178.4 146.3 %reduce-scatter.8.cloned.1.call-start = ((), (), s32[]{:S(2)}) async-start(), calls=%async_computation.6 | async-start | bytes 5308416 | tf_op jit(solution)/shard_map/reduce_scatter | solution.py:124
  184.4 10.9 %copy-start.55 = (f32[1,96]{1,0:T(1,128)S(1)}, f32[1,96]{1,0:T(1,128)}, u32[]{:S(2)}) copy-start(f32[1,96]{1,0:T(1,128)} %param.31) | copy-start | bytes 1156
  185.3 13.4 %copy-start.29 = (f32[128]{0:T(128)S(1)}, f32[128]{0:T(128)}, u32[]{:S(2)}) copy-start(f32[128]{0:T(128)} %copy-done.27) | copy-start | bytes 1540
  185.3 13.4 %copy-start.34 = (f32[128]{0:T(128)S(1)}, f32[128]{0:T(128)}, u32[]{:S(2)}) copy-start(f32[128]{0:T(128)} %copy-done.32) | copy-start | bytes 1540
  185.4 55.9 %all-to-all-start = ((bf16[128,8,384]{2,0,1:T(8,128)(2,1)}), bf16[128,8,384]{2,0,1:T(8,128)(2,1)S(1)}, u32[]{:S(2)}, u32[]{:S(2)}) async-start(bf16[128,8,384]{2,0,1:T(8,128)(2,1)} %bitcast.145), calls=%async_computation.3 | async-start | bytes 1572864 | tf_op jit(solution)/shard_map/all_to_all | solution.py:278
  194.0 197.5 %all-reduce.22.cloned.1.call-start = ((), (), s32[]{:S(2)}) async-start(), calls=%async_computation.11 | async-start | bytes 3538944 | tf_op jit(solution)/shard_map/psum | solution.py:134
  198.7 42.5 %copy-start.1 = (bf16[1024,768]{1,0:T(8,128)(2,1)S(1)}, bf16[1024,768]{1,0:T(8,128)(2,1)}, u32[]{:S(2)}) copy-start(bf16[1024,768]{1,0:T(8,128)(2,1)} %all-gather.17.cloned.1.call-done) | copy-start | bytes 4718596
  242.9 85.0 %copy-start.47 = (bf16[1,96]{1,0:T(2,128)(2,1)S(1)}, bf16[1,96]{1,0:T(2,128)(2,1)}, u32[]{:S(2)}) copy-start(bf16[1,96]{1,0:T(2,128)(2,1)} %convert_bitcast_fusion.1) | copy-start | bytes 580
  242.9 100.1 %copy-start.41 = (bf16[768]{0:T(1024)(128)(2,1)S(1)}, bf16[768]{0:T(1024)(128)(2,1)}, u32[]{:S(2)}) copy-start(bf16[768]{0:T(1024)(128)(2,1)} %get-tuple-element.72) | copy-start | bytes 4612
  242.9 100.1 %copy-start.46 = (f32[128]{0:T(128)S(1)}, f32[128]{0:T(128)}, u32[]{:S(2)}) copy-start(f32[128]{0:T(128)} %copy-done.45) | copy-start | bytes 1540
  242.9 100.1 %copy-start.56 = (f32[128]{0:T(128)S(1)}, f32[128]{0:T(128)}, u32[]{:S(2)}) copy-start(f32[128]{0:T(128)} %get-tuple-element.69) | copy-start | bytes 1540
  242.9 100.2 %copy-start.20 = (f32[128,768]{1,0:T(8,128)S(1)}, f32[128,768]{1,0:T(8,128)}, u32[]{:S(2)}) copy-start(f32[128,768]{1,0:T(8,128)} %get-tuple-element.120) | copy-start | bytes 1179652
  242.9 100.4 %copy-start.6 = (f32[128,768]{1,0:T(8,128)S(1)}, f32[128,768]{1,0:T(8,128)}, u32[]{:S(2)}) copy-start(f32[128,768]{1,0:T(8,128)} %copy-done.5) | copy-start | bytes 1179652
  242.9 100.4 %copy-start.40 = (f32[128]{0:T(128)S(1)}, f32[128]{0:T(128)}, u32[]{:S(2)}) copy-start(f32[128]{0:T(128)} %copy-done.39) | copy-start | bytes 1540
  324.8 19.4 %copy-start.12 = (bf16[128,3072]{1,0:T(8,128)(2,1)S(1)}, bf16[128,3072]{1,0:T(8,128)(2,1)}, u32[]{:S(2)}) copy-start(bf16[128,3072]{1,0:T(8,128)(2,1)} %get-tuple-element.115) | copy-start | bytes 2359300
  (27 other events, 66.7 us)
Sparse Core Ops, SparseCore 0:
  10.2 58.5 all-gather.18
  71.1 25.9 all-gather.20
  99.3 56.7 all-gather.22
  158.1 24.0 all-gather.16
  184.9 35.5 reduce-scatter.5
  222.7 46.2 reduce-scatter.3
  271.3 53.3 reduce-scatter.7
  328.8 62.6 all-reduce.21
